TPU v7x, 32 devices: a whole 2x2x4 slice. The times are simulated.
32 devices in a mesh: prow: 4 (over z), pcol: 8 (over y, x, core).
Axes of the slice: x: 2, y: 2, z: 4, core: 2. Of those that a mesh axis runs over, the one named last changes fastest.
Arguments:
- anc_inverse: float32 [2048, 2048], P('pcol', 'prow')
- pattern_one: int32 [8, 4], replicated, may hold values from 0 to 7, as said below
- parents: int32 [8], replicated, may hold values from 0 to 7, as said below
- low_one: float32 [8, 1024, 256], P('pcol', 'prow'), may hold values from -2 to 2
- pivot_one: float32 [8, 256, 256], P('pcol'), may hold values from -4 to 4
- low_two: float32 [8, 1024, 256], P('pcol', 'prow'), may hold values from -2 to 2
- second_scaled_factor: float32 [8, 256, 256], P('pcol'), may hold values from -2 to 2
- second_pivot_inverse: float32 [8, 256, 256], P('pcol'), may hold values from -4 to 4
Outputs:
- column_one: float32 [8, 2048, 256], P('prow', 'pcol')
- diag_one: float32 [8, 256, 256], P('pcol')
- column_two: float32 [8, 2048, 256], P('prow', 'pcol')
- second_parent_inverse: float32 [8, 256, 256], P('pcol')
- second_diagonal_inverse: float32 [8, 256, 256], P('pcol')
Inputs may be any that keep to these rules, and one draw needn't show every extreme that they name: `pattern_one`: entry r of each row names an ancestor of process row r: it lies in r * 2 to r * 2 + 1; for each r, every ancestor of that range is entry r of exactly 4 rows. `parents`: every first-level supernode is the parent of exactly one second-level supernode.
All inputs are finite; a program needn't handle non-finite values.
Results may differ from a plain program's by a relative error of at most 0.000073.
Values sent between devices are 32-bit elements; how exact they have to be, the bound alone decides.
A program may use at most 128 MiB of HBM per device.

v0:
```python
import jax
import jax.numpy as jnp
from jax import lax
from jax.sharding import PartitionSpec as P


def batched(left, right):
    return jnp.einsum("kab,kbd->kad", left, right, precision=lax.Precision.HIGHEST)


def batched_left_t(left, right):
    return jnp.einsum("kba,kbd->kad", left, right, precision=lax.Precision.HIGHEST)


def pick_rows(hit_mask, count):
    total = hit_mask.shape[0]
    keys = jnp.where(hit_mask, 0, total).astype(jnp.int32) + jnp.arange(total, dtype=jnp.int32)
    chosen_rows = jnp.argsort(keys)[:count]
    valid = jnp.take(hit_mask, chosen_rows, axis=0).astype(jnp.float32)[:, None, None]
    return (chosen_rows, valid)


def body(
    anc_inverse,
    pattern_one,
    parents,
    low_one,
    pivot_one,
    low_two,
    second_scaled_factor,
    second_pivot_inverse,
):
    my_row = lax.axis_index("prow")
    my_col = lax.axis_index("pcol")
    row_count = lax.axis_size("prow")
    col_count = lax.axis_size("pcol")
    per_row_anc = col_count // row_count
    supernode_block_width = pivot_one.shape[1]
    per_col_one = pivot_one.shape[0]
    per_col_two = second_scaled_factor.shape[0]
    owned = anc_inverse.shape[1] // supernode_block_width
    zblocks = anc_inverse.reshape(supernode_block_width, owned, supernode_block_width).transpose(
        1, 0, 2
    )
    lowall = lax.all_gather(low_one, "pcol", axis=0, tiled=True)
    total_one = lowall.shape[0]
    owned_slot_list = lax.dynamic_index_in_dim(pattern_one, my_row, 1, keepdims=False)
    chosen = jnp.take(zblocks, owned_slot_list - my_row * owned, axis=0)
    first_terms = batched(chosen, lowall)
    lowsec, topall = (
        lax.all_gather(low_two, "pcol", axis=0, tiled=True),
        lax.all_gather(second_scaled_factor, "pcol", axis=0, tiled=True),
    )
    total_two = lowsec.shape[0]
    pattern_two = jnp.take(pattern_one, parents, axis=0)
    my_slots_two = lax.dynamic_index_in_dim(pattern_two, my_row, 1, keepdims=False)
    chosen_two = jnp.take(zblocks, my_slots_two - my_row * owned, axis=0)
    first_full = -lax.psum(first_terms, "prow")
    share = total_two // row_count
    start = my_row * share
    parents_share = lax.dynamic_slice_in_dim(parents, start, share, 0)
    tops_share = lax.dynamic_slice_in_dim(topall, start, share, 0)
    carried = batched(jnp.take(first_full, parents_share, axis=0), tops_share)
    base_terms = batched(chosen_two, lowsec)
    updated = lax.dynamic_slice_in_dim(base_terms, start, share, 0) + carried
    second_terms = lax.dynamic_update_slice_in_dim(base_terms, updated, start, 0)
    second_full = -lax.psum(second_terms, "prow")
    rows_one, valid_one = pick_rows(owned_slot_list == my_col, total_one // per_row_anc)
    pivot_small = valid_one * batched_left_t(
        jnp.take(lowall, rows_one, axis=0), jnp.take(first_full, rows_one, axis=0)
    )
    pivot_terms = jnp.zeros_like(first_full).at[rows_one].add(pivot_small)
    pivot_part = lax.psum_scatter(pivot_terms, "pcol", scatter_dimension=0, tiled=True)
    pivot_sum = lax.psum(pivot_part, "prow")
    diag_one = pivot_one - pivot_sum
    count_one = first_full.shape[0] // row_count
    column_one = lax.dynamic_slice_in_dim(first_full, my_row * count_one, count_one, 0)
    second_level_count = second_full.shape[0] // row_count
    column_two = lax.dynamic_slice_in_dim(
        second_full, my_row * second_level_count, second_level_count, 0
    )
    rows_two, valid_two = pick_rows(my_slots_two == my_col, total_two // per_row_anc)
    lows_picked = jnp.take(lowsec, rows_two, axis=0)
    parent_picked = jnp.take(first_full, jnp.take(parents, rows_two, axis=0), axis=0)
    cross_small = valid_two * batched_left_t(parent_picked, lows_picked)
    diag_small = valid_two * batched_left_t(lows_picked, jnp.take(second_full, rows_two, axis=0))
    local_parent = parents - my_col * per_col_one
    own_parent = (local_parent >= 0) & (local_parent < per_col_one)
    rows_own, valid_own = pick_rows(own_parent, per_col_two)
    valid_own = valid_own * (my_row == 0).astype(jnp.float32)
    local_picked = jnp.clip(jnp.take(local_parent, rows_own, axis=0), 0, per_col_one - 1)
    picked = jnp.take(diag_one, local_picked, axis=0)
    own_small = valid_own * batched(picked, jnp.take(topall, rows_own, axis=0))
    cross_terms = (
        jnp.zeros_like(second_full).at[rows_two].add(cross_small).at[rows_own].add(own_small)
    )
    diag_terms = jnp.zeros_like(second_full).at[rows_two].add(diag_small)
    part_cross, part_diag = (
        lax.psum_scatter(cross_terms, "pcol", scatter_dimension=0, tiled=True),
        lax.psum_scatter(diag_terms, "pcol", scatter_dimension=0, tiled=True),
    )
    sum_cross, sum_diag = lax.psum((part_cross, part_diag), "prow")
    second_parent_inverse = -sum_cross
    second_diagonal_inverse = (
        second_pivot_inverse
        - batched_left_t(second_scaled_factor, second_parent_inverse)
        - sum_diag
    )
    return (column_one, diag_one, column_two, second_parent_inverse, second_diagonal_inverse)


def solution(mesh):
    placed = (
        P("pcol", "prow"),
        P(),
        P(),
        P("pcol", "prow", None),
        P("pcol", None, None),
        P("pcol", "prow", None),
        P("pcol", None, None),
        P("pcol", None, None),
    )
    return jax.shard_map(
        body,
        mesh=mesh,
        in_specs=placed,
        out_specs=(
            P("prow", "pcol", None),
            P("pcol", None, None),
            P("prow", "pcol", None),
            P("pcol", None, None),
            P("pcol", None, None),
        ),
        check_vma=False,
    )
```

profile of v0, /device:TPU:0, one launch (start us, length us, event | category | flops | bytes accessed | tf_op | source)
XLA Modules:
  0.0 471.5 jit_solution(3958737760766188225)
XLA Ops:
  10.5 30.0 %all-gather.4.cloned.1.call-done = f32[8,256,256]{2,1,0:T(8,128)} async-done(((f32[1,256,256]{2,1,0:T(8,128)}), f32[8,256,256]{2,1,0:T(8,128)}) %all-gather.4.cloned.1.call-update) | async-done | bytes 2097168 | tf_op jit(solution)/shard_map/all_gather | solution.py:45
  40.4 5.1 %fusion.2 = f32[8,256,256]{2,1,0:T(8,128)} fusion(f32[8,256,256]{2,1,0:T(8,128)} %all-gather.4.cloned.1.call-done, f32[8,256,256]{2,1,0:T(8,128)S(1)} %gather_fusion.3, pred[8]{0:T(512)(128)(4,1)S(1)} %compare_and_fusion.4), kind=kOutput, calls=%fused_computation.17 | convolution fusion | flops 1611137024 | bytes 6291464 | tf_op jit(solution)/shard_map/kab,kbd->kad/dot_general | solution.py:8
  50.4 81.4 %all-reduce.6.cloned.1.call-done = f32[8,256,256]{2,1,0:T(8,128)} async-done(((f32[8,256,256]{2,1,0:T(8,128)}), f32[8,256,256]{2,1,0:T(8,128)}) %all-reduce.6.cloned.1.call-update) | async-done | bytes 2097168 | tf_op jit(solution)/shard_map/psum | solution.py:58
  135.3 4.5 convolution_multiply_fusion.2
  140.0 2.3 scatter_fusion
  144.8 2.0 gather_fusion.7
  146.9 13.7 %all-gather.6.cloned.1.call-done = f32[8,256,256]{2,1,0:T(8,128)} async-done(((f32[1,256,256]{2,1,0:T(8,128)}), f32[8,256,256]{2,1,0:T(8,128)}) %all-gather.6.cloned.1.call-update) | async-done | bytes 2097168 | tf_op jit(solution)/shard_map/all_gather | solution.py:51
  160.6 5.8 %fusion = f32[8,256,256]{2,1,0:T(8,128)} fusion(f32[8,256,256]{2,1,0:T(8,128)} %all-gather.6.cloned.1.call-done, f32[8,256,256]{2,1,0:T(8,128)} %gather_fusion.7, pred[8]{0:T(512)(128)(4,1)S(1)} %compare_and_fusion.2), kind=kOutput, calls=%fused_computation.15 | convolution fusion | flops 1611137024 | bytes 6291464 | tf_op jit(solution)/shard_map/kab,kbd->kad/dot_general | solution.py:8
  166.9 23.2 %all-gather.8.cloned.1.call-done = f32[8,256,256]{2,1,0:T(8,128)} async-done(((f32[1,256,256]{2,1,0:T(8,128)}), f32[8,256,256]{2,1,0:T(8,128)}) %all-gather.8.cloned.1.call-update) | async-done | bytes 2097168 | tf_op jit(solution)/shard_map/all_gather | solution.py:52
  190.1 2.7 fusion.4
  192.9 41.5 %reduce-scatter.4.cloned.1.call-done = f32[1,256,256]{2,1,0:T(8,128)} async-done(((f32[8,256,256]{2,1,0:T(8,128)}), f32[1,256,256]{2,1,0:T(8,128)}) %reduce-scatter.4.cloned.1.call-update) | async-done | bytes 262160 | tf_op jit(solution)/shard_map/reduce_scatter | solution.py:73
  241.2 2.6 gather_fusion.10
  245.3 4.2 convolution_multiply_fusion.1
  249.8 2.3 scatter_fusion.1
  252.1 79.3 %all-reduce.10.cloned.1.call-done = (f32[1,256,256]{2,1,0:T(8,128)}, f32[8,256,256]{2,1,0:T(8,128)}) async-done(((f32[1,256,256]{2,1,0:T(8,128)}, f32[8,256,256]{2,1,0:T(8,128)}), (f32[1,256,256]{2,1,0:T(8,128)}, f32[8,256,256]{2,1,0:T(8,128)})) %all-reduce.10.cloned.1.call-update) | async-done | bytes 2359312 | tf_op jit(solution)/shard_map/psum | solution.py:74
  332.5 2.0 fusion.8
  335.9 1.8 neg.10
  339.4 4.3 convolution_multiply_fusion
  347.7 28.5 %reduce-scatter.6.cloned.1.call-done = f32[1,256,256]{2,1,0:T(8,128)} async-done(((f32[8,256,256]{2,1,0:T(8,128)}), f32[1,256,256]{2,1,0:T(8,128)}) %reduce-scatter.6.cloned.1.call-update) | async-done | bytes 262160 | tf_op jit(solution)/shard_map/reduce_scatter | solution.py:99
  376.2 44.4 %reduce-scatter.8.cloned.1.call-done = f32[1,256,256]{2,1,0:T(8,128)} async-done(((f32[8,256,256]{2,1,0:T(8,128)}), f32[1,256,256]{2,1,0:T(8,128)}) %reduce-scatter.8.cloned.1.call-update) | async-done | bytes 262160 | tf_op jit(solution)/shard_map/reduce_scatter | solution.py:100
  420.6 1.9 constant_dynamic-slice_fusion.1
  422.5 1.9 constant_dynamic-slice_fusion
  424.3 37.3 %all-reduce.8.cloned.1.call-done = (f32[1,256,256]{2,1,0:T(8,128)}, f32[1,256,256]{2,1,0:T(8,128)}) async-done(((f32[1,256,256]{2,1,0:T(8,128)}, f32[1,256,256]{2,1,0:T(8,128)}), (f32[1,256,256]{2,1,0:T(8,128)}, f32[1,256,256]{2,1,0:T(8,128)})) %all-reduce.8.cloned.1.call-update) | async-done | bytes 524304 | tf_op jit(solution)/shard_map/psum | solution.py:102
  462.6 2.3 fusion.10
  (101 shorter events, 30.8 us)
Async XLA Ops:
  7.2 2.3 copy-start.13
  7.2 2.5 copy-start
  7.2 33.2 %all-gather.4.cloned.1.call-start = ((), (), s32[]{:S(2)}) async-start(), calls=%async_computation.3 | async-start | bytes 2359296 | tf_op jit(solution)/shard_map/all_gather | solution.py:45
  7.9 123.9 %all-reduce.6.cloned.1.call-start = ((), (), s32[]{:S(2)}) async-start(), calls=%async_computation.4 | async-start | bytes 4194304 | tf_op jit(solution)/shard_map/psum | solution.py:58
  45.5 3.2 copy-start.7
  45.5 115.0 %all-gather.6.cloned.1.call-start = ((), (), s32[]{:S(2)}) async-start(), calls=%async_computation.6 | async-start | bytes 2359296 | tf_op jit(solution)/shard_map/all_gather | solution.py:51
  46.3 143.9 %all-gather.8.cloned.1.call-start = ((), (), s32[]{:S(2)}) async-start(), calls=%async_computation.7 | async-start | bytes 2359296 | tf_op jit(solution)/shard_map/all_gather | solution.py:52
  46.9 187.5 %reduce-scatter.4.cloned.1.call-start = ((), (), s32[]{:S(2)}) async-start(), calls=%async_computation.5 | async-start | bytes 2359296 | tf_op jit(solution)/shard_map/reduce_scatter | solution.py:73
  133.6 1.7 copy-start.4
  142.3 1.3 copy-start.3
  143.7 187.7 %all-reduce.10.cloned.1.call-start = ((), (), s32[]{:S(2)}) async-start(), calls=%async_computation.11 | async-start | bytes 4718592 | tf_op jit(solution)/shard_map/psum | solution.py:74
  146.9 19.5 %copy-start.5 = (f32[8,256,256]{2,1,0:T(8,128)S(1)}, f32[8,256,256]{2,1,0:T(8,128)}, u32[]{:S(2)}) copy-start(f32[8,256,256]{2,1,0:T(8,128)} %copy-done.4) | copy-start | bytes 6291460
  192.9 47.6 %copy-start.14 = (s32[3]{0:T(128)S(1)}, s32[3]{0:T(128)}, u32[]{:S(2)}) copy-start(s32[3]{0:T(128)} %constant.171.clone.1) | copy-start | bytes 40
  234.4 141.8 %reduce-scatter.6.cloned.1.call-start = ((), (), s32[]{:S(2)}) async-start(), calls=%async_computation.8 | async-start | bytes 2359296 | tf_op jit(solution)/shard_map/reduce_scatter | solution.py:99
  332.5 5.2 %copy-start.9 = (f32[1,256,256]{2,1,0:T(8,128)}, f32[1,256,256]{2,1,0:T(8,128)S(1)}, u32[]{:S(2)}) copy-start(f32[1,256,256]{2,1,0:T(8,128)S(1)} %sub.32) | copy-start | bytes 786436
  334.5 1.3 copy-start.1
  335.9 84.7 %reduce-scatter.8.cloned.1.call-start = ((), (), s32[]{:S(2)}) async-start(), calls=%async_computation.9 | async-start | bytes 2359296 | tf_op jit(solution)/shard_map/reduce_scatter | solution.py:100
  337.7 1.7 copy-start.6
  343.7 1.3 copy-start.8
  346.2 1.3 copy-start.2
  347.6 115.0 %copy-start.10 = (f32[1,256,256]{2,1,0:T(8,128)S(1)}, f32[1,256,256]{2,1,0:T(8,128)}, u32[]{:S(2)}) copy-start(f32[1,256,256]{2,1,0:T(8,128)} %param.22) | copy-start | bytes 786436
  347.6 115.0 %copy-start.12 = (f32[1,256,256]{2,1,0:T(8,128)S(1)}, f32[1,256,256]{2,1,0:T(8,128)}, u32[]{:S(2)}) copy-start(f32[1,256,256]{2,1,0:T(8,128)} %param.23) | copy-start | bytes 786436
  347.6 114.0 %all-reduce.8.cloned.1.call-start = ((), (), s32[]{:S(2)}) async-start(), calls=%async_computation.10 | async-start | bytes 1048576 | tf_op jit(solution)/shard_map/psum | solution.py:102
  462.6 2.4 copy-start.11
Sparse Core Ops, SparseCore 0:
  9.9 30.4 all-gather.3
  45.7 86.1 all-reduce.5
  133.7 26.8 all-gather.5
  162.3 27.7 all-gather.7
  193.3 41.0 reduce-scatter.3
  236.7 94.6 all-reduce.9
  336.0 40.1 reduce-scatter.5
  379.5 41.0 reduce-scatter.7
  423.0 38.6 all-reduce.7
where the time goes:
time: 472 us
  waiting for transfers between devices  381 us (81%)
  matrix products  31 us (7%)
  local copies, waits for them, and re-layouts  27 us (6%)
  other arithmetic  16 us (3%)
  between operations  15.6 us (3%)
    psum x1, waiting for transfers between devices, body(): first_full = -lax.psum(first_terms, 'prow')  81.4 us
    psum x1, waiting for transfers between devices, body(): pivot_sum = lax.psum(pivot_part, 'prow')  79.3 us
    reduce_scatter x1, waiting for transfers between devices, body(): lax.psum_scatter(diag_terms, 'pcol', scatter_dimension=0, tiled=True)  44.4 us
    reduce_scatter x1, waiting for transfers between devices, body(): lax.psum_scatter(pivot_terms, 'pcol', scatter_dimension=0, tiled=True)  41.5 us
    psum x1, waiting for transfers between devices, body(): sum_cross, sum_diag = lax.psum((part_cross, part_diag), 'prow')  37.3 us
    all_gather x1, waiting for transfers between devices, body(): lowall = lax.all_gather(low_one, 'pcol', axis=0, tiled=True)  30 us
    reduce_scatter x1, waiting for transfers between devices, body(): lax.psum_scatter(cross_terms, 'pcol', scatter_dimension=0, tiled=True)  28.5 us
    all_gather x1, waiting for transfers between devices, body(): lax.all_gather(second_scaled_factor, 'pcol', axis=0, tiled=True)  23.2 us
  transfers between devices with their start and end apart: 9, of which 9 were waited for; matrix products, arithmetic and copies ran while one was open for 12% of the time, Pallas kernels for 0%

commit v1 on v0

--- a/solution.py
+++ b/solution.py
@@ -42,7 +42,12 @@
     zblocks = anc_inverse.reshape(supernode_block_width, owned, supernode_block_width).transpose(
         1, 0, 2
     )
-    lowall = lax.all_gather(low_one, "pcol", axis=0, tiled=True)
+    ring = [low_one]
+    for hop in range(7):
+        ring.append(lax.ppermute(ring[-1], "pcol", [(dev, (dev + 1) % 8) for dev in range(8)]))
+    lowall = jnp.roll(
+        jnp.concatenate(ring[::-1], axis=0), (lax.axis_index("pcol") + 1) * ring[0].shape[0], axis=0
+    )
     total_one = lowall.shape[0]
     owned_slot_list = lax.dynamic_index_in_dim(pattern_one, my_row, 1, keepdims=False)
     chosen = jnp.take(zblocks, owned_slot_list - my_row * owned, axis=0)

time: 472 us -> 435 us (0.922)
  waiting for transfers between devices: 381 us -> 339 us
  local copies, waits for them, and re-layouts: 27 us -> 31.9 us
    ppermute x0 -> x7, waiting for transfers between devices: none -> 42.2 us  [body(): lax.ppermute(ring[-1], 'pcol', [(dev, (dev + 1) % 8) for dev in range(8)])]
    all_gather x1 -> x0, waiting for transfers between devices: 30 us -> none  [body(): lowall = lax.all_gather(low_one, 'pcol', axis=0, tiled=True)]
    all_gather x1, waiting for transfers between devices: 23.2 us -> 0.03 us  [body(): lax.all_gather(second_scaled_factor, 'pcol', axis=0, tiled=True)]
    reduce_scatter x1, waiting for transfers between devices: 41.5 us -> 27.4 us  [body(): lax.psum_scatter(pivot_terms, 'pcol', scatter_dimension=0, tiled=True)]
    all_gather x1, waiting for transfers between devices: 13.7 us -> 0.03 us  [body(): lax.all_gather(low_two, 'pcol', axis=0, tiled=True)]
  transfers between devices with their start and end apart: 9 -> 15, of which waited for: 9 -> 13; matrix products, arithmetic and copies ran while one was open for 12% -> 14% of each run, Pallas kernels for 0% -> 0%
where the time goes in v1:
time: 435 us; the launch traced here: 434 us
  waiting for transfers between devices  339 us (78%)
  local copies, waits for them, and re-layouts  31.9 us (7%)
  matrix products  29 us (7%)
  between operations  17.4 us (4%)
  other arithmetic  15.5 us (4%)
    psum x1, waiting for transfers between devices, body(): first_full = -lax.psum(first_terms, 'prow')  82.6 us
    psum x1, waiting for transfers between devices, body(): pivot_sum = lax.psum(pivot_part, 'prow')  78.4 us
    reduce_scatter x1, waiting for transfers between devices, body(): lax.psum_scatter(diag_terms, 'pcol', scatter_dimension=0, tiled=True)  44.3 us
    ppermute x7, waiting for transfers between devices, body(): lax.ppermute(ring[-1], 'pcol', [(dev, (dev + 1) % 8) for dev in range(8)])  42.2 us
    psum x1, waiting for transfers between devices, body(): sum_cross, sum_diag = lax.psum((part_cross, part_diag), 'prow')  35 us
    reduce_scatter x1, waiting for transfers between devices, body(): lax.psum_scatter(cross_terms, 'pcol', scatter_dimension=0, tiled=True)  28.1 us
    reduce_scatter x1, waiting for transfers between devices, body(): lax.psum_scatter(pivot_terms, 'pcol', scatter_dimension=0, tiled=True)  27.4 us
    dot_general x4, matrix products, batched_left_t(): jnp.einsum('kba,kbd->kad', left, right, precision=lax.Precision.HIGHEST)  14.6 us
  transfers between devices with their start and end apart: 15, of which 13 were waited for; matrix products, arithmetic and copies ran while one was open for 14% of the time, Pallas kernels for 0%

profile of v1, /device:TPU:0, one launch (start us, length us, event | category | flops | bytes accessed | tf_op | source)
XLA Modules:
  0.0 434.0 jit_solution(2823523064971785174)
XLA Ops:
  8.6 7.1 %collective-permute-done = f32[1,256,256]{2,1,0:T(8,128)S(1)} collective-permute-done((f32[1,256,256]{2,1,0:T(8,128)}, f32[1,256,256]{2,1,0:T(8,128)S(1)}, u32[]{:S(2)}, u32[]{:S(2)}) %collective-permute-start) | collective-permute-done | bytes 262176 | tf_op jit(solution)/shard_map/ppermute | solution.py:47
  15.7 6.7 %collective-permute-done.1 = f32[1,256,256]{2,1,0:T(8,128)S(1)} collective-permute-done((f32[1,256,256]{2,1,0:T(8,128)S(1)}, f32[1,256,256]{2,1,0:T(8,128)S(1)}, u32[]{:S(2)}, u32[]{:S(2)}) %collective-permute-start.1) | collective-permute-done | bytes 262176 | tf_op jit(solution)/shard_map/ppermute | solution.py:47
  22.4 6.7 %collective-permute-done.2 = f32[1,256,256]{2,1,0:T(8,128)S(1)} collective-permute-done((f32[1,256,256]{2,1,0:T(8,128)S(1)}, f32[1,256,256]{2,1,0:T(8,128)S(1)}, u32[]{:S(2)}, u32[]{:S(2)}) %collective-permute-start.2) | collective-permute-done | bytes 262176 | tf_op jit(solution)/shard_map/ppermute | solution.py:47
  29.1 6.7 %collective-permute-done.3 = f32[1,256,256]{2,1,0:T(8,128)S(1)} collective-permute-done((f32[1,256,256]{2,1,0:T(8,128)S(1)}, f32[1,256,256]{2,1,0:T(8,128)S(1)}, u32[]{:S(2)}, u32[]{:S(2)}) %collective-permute-start.3) | collective-permute-done | bytes 262176 | tf_op jit(solution)/shard_map/ppermute | solution.py:47
  35.8 6.7 %collective-permute-done.4 = f32[1,256,256]{2,1,0:T(8,128)S(1)} collective-permute-done((f32[1,256,256]{2,1,0:T(8,128)S(1)}, f32[1,256,256]{2,1,0:T(8,128)S(1)}, u32[]{:S(2)}, u32[]{:S(2)}) %collective-permute-start.4) | collective-permute-done | bytes 262176 | tf_op jit(solution)/shard_map/ppermute | solution.py:47
  44.1 5.1 %collective-permute-done.5 = f32[1,256,256]{2,1,0:T(8,128)S(1)} collective-permute-done((f32[1,256,256]{2,1,0:T(8,128)S(1)}, f32[1,256,256]{2,1,0:T(8,128)S(1)}, u32[]{:S(2)}, u32[]{:S(2)}) %collective-permute-start.5) | collective-permute-done | bytes 262176 | tf_op jit(solution)/shard_map/ppermute | solution.py:47
  50.7 2.0 gather_fusion.3
  52.7 3.2 collective-permute-done.6
  57.9 3.5 fusion.2
  66.2 82.6 %all-reduce.6.cloned.1.call-done = f32[8,256,256]{2,1,0:T(8,128)} async-done(((f32[8,256,256]{2,1,0:T(8,128)}), f32[8,256,256]{2,1,0:T(8,128)}) %all-reduce.6.cloned.1.call-update) | async-done | bytes 2097168 | tf_op jit(solution)/shard_map/psum | solution.py:63
  152.3 4.5 %convolution_multiply_fusion.2 = f32[4,256,256]{2,1,0:T(8,128)} fusion(f32[4,256,256]{2,1,0:T(8,128)} %gather_fusion.6, f32[4,256,256]{2,1,0:T(8,128)} %gather_fusion.5, f32[4]{0:T(128)S(1)} %select_convert_fusion.1, pred[4]{0:T(512)(128)(4,1)S(1)} %get-tuple-element.71), kind=kOutput, calls=%fused_computation.21 | convolution fusion | flops 806092800 | bytes 3145748 | tf_op jit(solution)/shard_map/kba,kbd->kad/dot_general | solution.py:12
  157.0 2.3 scatter_fusion
  163.9 6.1 %fusion = f32[8,256,256]{2,1,0:T(8,128)} fusion(f32[8,256,256]{2,1,0:T(8,128)} %all-gather.3.cloned.1.call-done, f32[8,256,256]{2,1,0:T(8,128)} %gather_fusion.7, pred[8]{0:T(512)(128)(4,1)S(1)} %compare_and_fusion.2), kind=kOutput, calls=%fused_computation.15 | convolution fusion | flops 1611137024 | bytes 6291464 | tf_op jit(solution)/shard_map/kab,kbd->kad/dot_general | solution.py:8
  170.6 2.8 fusion.4
  173.4 27.4 %reduce-scatter.4.cloned.1.call-done = f32[1,256,256]{2,1,0:T(8,128)} async-done(((f32[8,256,256]{2,1,0:T(8,128)}), f32[1,256,256]{2,1,0:T(8,128)}) %reduce-scatter.4.cloned.1.call-update) | async-done | bytes 262160 | tf_op jit(solution)/shard_map/reduce_scatter | solution.py:78
  207.6 3.2 gather_fusion.10
  212.4 3.5 convolution_multiply_fusion.1
  217.2 78.4 %all-reduce.10.cloned.1.call-done = (f32[1,256,256]{2,1,0:T(8,128)}, f32[8,256,256]{2,1,0:T(8,128)}) async-done(((f32[1,256,256]{2,1,0:T(8,128)}, f32[8,256,256]{2,1,0:T(8,128)}), (f32[1,256,256]{2,1,0:T(8,128)}, f32[8,256,256]{2,1,0:T(8,128)})) %all-reduce.10.cloned.1.call-update) | async-done | bytes 2359312 | tf_op jit(solution)/shard_map/psum | solution.py:79
  296.7 2.0 fusion.8
  304.0 4.3 convolution_multiply_fusion
  312.1 28.1 %reduce-scatter.6.cloned.1.call-done = f32[1,256,256]{2,1,0:T(8,128)} async-done(((f32[8,256,256]{2,1,0:T(8,128)}), f32[1,256,256]{2,1,0:T(8,128)}) %reduce-scatter.6.cloned.1.call-update) | async-done | bytes 262160 | tf_op jit(solution)/shard_map/reduce_scatter | solution.py:104
  340.2 44.3 %reduce-scatter.8.cloned.1.call-done = f32[1,256,256]{2,1,0:T(8,128)} async-done(((f32[8,256,256]{2,1,0:T(8,128)}), f32[1,256,256]{2,1,0:T(8,128)}) %reduce-scatter.8.cloned.1.call-update) | async-done | bytes 262160 | tf_op jit(solution)/shard_map/reduce_scatter | solution.py:105
  388.3 35.0 %all-reduce.8.cloned.1.call-done = (f32[1,256,256]{2,1,0:T(8,128)}, f32[1,256,256]{2,1,0:T(8,128)}) async-done(((f32[1,256,256]{2,1,0:T(8,128)}, f32[1,256,256]{2,1,0:T(8,128)}), (f32[1,256,256]{2,1,0:T(8,128)}, f32[1,256,256]{2,1,0:T(8,128)})) %all-reduce.8.cloned.1.call-update) | async-done | bytes 524304 | tf_op jit(solution)/shard_map/psum | solution.py:107
  424.3 2.3 fusion.10
  (131 shorter events, 42.1 us)
Async XLA Ops:
  8.0 140.8 %all-reduce.6.cloned.1.call-start = ((), (), s32[]{:S(2)}) async-start(), calls=%async_computation.3 | async-start | bytes 4194304 | tf_op jit(solution)/shard_map/psum | solution.py:63
  8.0 7.7 %collective-permute-start = (f32[1,256,256]{2,1,0:T(8,128)}, f32[1,256,256]{2,1,0:T(8,128)S(1)}, u32[]{:S(2)}, u32[]{:S(2)}) collective-permute-start(f32[1,256,256]{2,1,0:T(8,128)} %param.19), channel_id=1, source_target_pairs={{0,1},{1,2},{2,3},{3,4},{4,5},{5,6},{6,7},{7,0},{8,9},{9,10},{10,1... | collective-permute-start | bytes 786440 | tf_op jit(solution)/shard_map/ppermute | solution.py:47
  15.7 6.7 %collective-permute-start.1 = (f32[1,256,256]{2,1,0:T(8,128)S(1)}, f32[1,256,256]{2,1,0:T(8,128)S(1)}, u32[]{:S(2)}, u32[]{:S(2)}) collective-permute-start(f32[1,256,256]{2,1,0:T(8,128)S(1)} %collective-permute-done), channel_id=1, source_target_pairs={{0,1},{1,2},{2,3},{3,4},{4,5},{5,6},{6,7},{7,0},{8,9},{9,10},{10,1... | collective-permute-start | bytes 786440 | tf_op jit(solution)/shard_map/ppermute | solution.py:47
  22.4 6.7 %collective-permute-start.2 = (f32[1,256,256]{2,1,0:T(8,128)S(1)}, f32[1,256,256]{2,1,0:T(8,128)S(1)}, u32[]{:S(2)}, u32[]{:S(2)}) collective-permute-start(f32[1,256,256]{2,1,0:T(8,128)S(1)} %collective-permute-done.1), channel_id=1, source_target_pairs={{0,1},{1,2},{2,3},{3,4},{4,5},{5,6},{6,7},{7,0},{8,9},{9,10},{10,1... | collective-permute-start | bytes 786440 | tf_op jit(solution)/shard_map/ppermute | solution.py:47
  29.1 6.7 %collective-permute-start.3 = (f32[1,256,256]{2,1,0:T(8,128)S(1)}, f32[1,256,256]{2,1,0:T(8,128)S(1)}, u32[]{:S(2)}, u32[]{:S(2)}) collective-permute-start(f32[1,256,256]{2,1,0:T(8,128)S(1)} %collective-permute-done.2), channel_id=1, source_target_pairs={{0,1},{1,2},{2,3},{3,4},{4,5},{5,6},{6,7},{7,0},{8,9},{9,10},{10,1... | collective-permute-start | bytes 786440 | tf_op jit(solution)/shard_map/ppermute | solution.py:47
  35.8 6.7 %collective-permute-start.4 = (f32[1,256,256]{2,1,0:T(8,128)S(1)}, f32[1,256,256]{2,1,0:T(8,128)S(1)}, u32[]{:S(2)}, u32[]{:S(2)}) collective-permute-start(f32[1,256,256]{2,1,0:T(8,128)S(1)} %collective-permute-done.3), channel_id=1, source_target_pairs={{0,1},{1,2},{2,3},{3,4},{4,5},{5,6},{6,7},{7,0},{8,9},{9,10},{10,1... | collective-permute-start | bytes 786440 | tf_op jit(solution)/shard_map/ppermute | solution.py:47
  42.5 6.7 %collective-permute-start.5 = (f32[1,256,256]{2,1,0:T(8,128)S(1)}, f32[1,256,256]{2,1,0:T(8,128)S(1)}, u32[]{:S(2)}, u32[]{:S(2)}) collective-permute-start(f32[1,256,256]{2,1,0:T(8,128)S(1)} %collective-permute-done.4), channel_id=1, source_target_pairs={{0,1},{1,2},{2,3},{3,4},{4,5},{5,6},{6,7},{7,0},{8,9},{9,10},{10,1... | collective-permute-start | bytes 786440 | tf_op jit(solution)/shard_map/ppermute | solution.py:47
  49.2 6.7 %collective-permute-start.6 = (f32[1,256,256]{2,1,0:T(8,128)S(1)}, f32[1,256,256]{2,1,0:T(8,128)S(1)}, u32[]{:S(2)}, u32[]{:S(2)}) collective-permute-start(f32[1,256,256]{2,1,0:T(8,128)S(1)} %collective-permute-done.5), channel_id=1, source_target_pairs={{0,1},{1,2},{2,3},{3,4},{4,5},{5,6},{6,7},{7,0},{8,9},{9,10},{10,1... | collective-permute-start | bytes 786440 | tf_op jit(solution)/shard_map/ppermute | solution.py:47
  52.7 3.4 copy-start.13
  61.5 102.4 %all-gather.3.cloned.1.call-start = ((), (), s32[]{:S(2)}) async-start(), calls=%async_computation.5 | async-start | bytes 2359296 | tf_op jit(solution)/shard_map/all_gather | solution.py:56
  62.1 108.6 %all-gather.5.cloned.1.call-start = ((), (), s32[]{:S(2)}) async-start(), calls=%async_computation.6 | async-start | bytes 2359296 | tf_op jit(solution)/shard_map/all_gather | solution.py:57
  62.6 138.1 %reduce-scatter.4.cloned.1.call-start = ((), (), s32[]{:S(2)}) async-start(), calls=%async_computation.4 | async-start | bytes 2359296 | tf_op jit(solution)/shard_map/reduce_scatter | solution.py:78
  157.0 3.8 copy-start
  160.7 135.0 %all-reduce.10.cloned.1.call-start = ((), (), s32[]{:S(2)}) async-start(), calls=%async_computation.10 | async-start | bytes 4718592 | tf_op jit(solution)/shard_map/psum | solution.py:79
  163.9 6.1 %copy-start.5 = (f32[8,256,256]{2,1,0:T(8,128)S(1)}, f32[8,256,256]{2,1,0:T(8,128)}, u32[]{:S(2)}) copy-start(f32[8,256,256]{2,1,0:T(8,128)} %copy-done.4) | copy-start | bytes 6291460
  173.4 33.5 %copy-start.15 = (s32[3]{0:T(128)S(1)}, s32[3]{0:T(128)}, u32[]{:S(2)}) copy-start(s32[3]{0:T(128)} %constant.191.clone.1) | copy-start | bytes 40
  200.8 139.4 %reduce-scatter.6.cloned.1.call-start = ((), (), s32[]{:S(2)}) async-start(), calls=%async_computation.7 | async-start | bytes 2359296 | tf_op jit(solution)/shard_map/reduce_scatter | solution.py:104
  296.7 5.2 %copy-start.10 = (f32[1,256,256]{2,1,0:T(8,128)}, f32[1,256,256]{2,1,0:T(8,128)S(1)}, u32[]{:S(2)}) copy-start(f32[1,256,256]{2,1,0:T(8,128)S(1)} %sub.37) | copy-start | bytes 786436
  300.1 84.4 %reduce-scatter.8.cloned.1.call-start = ((), (), s32[]{:S(2)}) async-start(), calls=%async_computation.8 | async-start | bytes 2359296 | tf_op jit(solution)/shard_map/reduce_scatter | solution.py:105
  301.9 2.0 copy-start.6
  312.0 112.3 %copy-start.11 = (f32[1,256,256]{2,1,0:T(8,128)S(1)}, f32[1,256,256]{2,1,0:T(8,128)}, u32[]{:S(2)}) copy-start(f32[1,256,256]{2,1,0:T(8,128)} %param.22) | copy-start | bytes 786436
  312.0 112.3 %copy-start.14 = (f32[1,256,256]{2,1,0:T(8,128)S(1)}, f32[1,256,256]{2,1,0:T(8,128)}, u32[]{:S(2)}) copy-start(f32[1,256,256]{2,1,0:T(8,128)} %param.23) | copy-start | bytes 786436
  312.1 111.3 %all-reduce.8.cloned.1.call-start = ((), (), s32[]{:S(2)}) async-start(), calls=%async_computation.9 | async-start | bytes 1048576 | tf_op jit(solution)/shard_map/psum | solution.py:107
  424.3 2.4 copy-start.12
  (7 other events, 10.2 us)
Sparse Core Ops, SparseCore 0:
  61.6 87.1 all-reduce.5
  200.9 94.6 all-reduce.9
  384.7 38.5 all-reduce.7
Sparse Core Ops, SparseCore 1:
  63.9 28.7 all-gather.2
  94.4 27.6 all-gather.4
  160.8 40.0 reduce-scatter.3
  300.2 40.0 reduce-scatter.5
  343.5 41.0 reduce-scatter.7
